TPU v7x, 512 devices: a whole 4x4x16 slice. The times are simulated.
512 devices in a mesh: layer: 4 (over y), dp: 4 (over x_lo, core), mp: 32 (over z, x_hi).
Axes of the slice: x: 4 (x_hi: 2, x_lo: 2; x = x_hi * 2 + x_lo), y: 4, z: 16, core: 2. Of those that a mesh axis runs over, the one named last changes fastest.
Arguments:
- mlp_in: bfloat16 [4, 128, 2048], P('layer', 'dp', 'mp'), may hold values from -6 to 6
- gate_weight: bfloat16 [4, 2048, 8192], P('layer', None, ('dp', 'mp')), may hold values from -0.125 to 0.125
- up_weight: bfloat16 [4, 2048, 8192], P('layer', None, ('dp', 'mp')), may hold values from -0.125 to 0.125
- down_weight: bfloat16 [4, 8192, 2048], P('layer', ('dp', 'mp')), may hold values from -0.0625 to 0.0625
- enc_weight: bfloat16 [4, 2048, 16384], P('layer', None, ('dp', 'mp')), may hold values from -0.125 to 0.125
- enc_bias: float32 [4, 16384], P('layer', ('dp', 'mp')), may hold values from -3 to 3
- dec_weight: bfloat16 [4, 4, 16384, 2048], P('layer', None, ('dp', 'mp')), may hold values from -0.046875 to 0.046875
Outputs:
- error_nodes: bfloat16 [4, 128, 2048], P('layer', 'dp', 'mp')
- latents: bfloat16 [4, 128, 16384], P('layer', None, ('dp', 'mp'))
All inputs are finite; a program needn't handle non-finite values.
Results may differ from a plain program's by a relative error of at most 0.0049.
Values may be sent and summed in bfloat16 or wider, within the bound.
No kernel may reach another device: no remote copies, remote signals or barrier semaphores. Data moves between devices by JAX's collectives and lax.ppermute only.
A program may use at most 64 MiB of HBM per device.

v0:
```python
import jax
import jax.numpy as jnp
from jax import lax
from jax.sharding import PartitionSpec as P


def choose_source(weights, source, layers):
    return lax.dynamic_index_in_dim(weights, jnp.clip(source, 0, layers - 1), 0, keepdims=False)


def body(mlp_in, gate_weight, up_weight, down_weight, enc_weight, enc_bias, dec_weight):
    layer_now = lax.axis_index("layer")
    layers = lax.axis_size("layer")
    features_full = lax.all_gather(mlp_in, "mp", axis=2, tiled=True)
    tok_rows = features_full.shape[1]
    width = features_full.shape[2]
    gathered = lax.all_gather(features_full.reshape(tok_rows, 1, width), "dp", axis=1, tiled=True)
    spread = gathered.shape[1]
    all_rows = gathered.reshape(tok_rows * spread, width)
    gate_part = jnp.dot(all_rows, gate_weight[0], preferred_element_type=jnp.float32)
    up_part = jnp.dot(all_rows, up_weight[0], preferred_element_type=jnp.float32)
    hidden = (jax.nn.silu(gate_part) * up_part).astype(jnp.bfloat16)
    pre_act = (
        jnp.dot(all_rows, enc_weight[0], preferred_element_type=jnp.float32) + enc_bias[0][None, :]
    )
    latent = jnp.maximum(pre_act, jnp.float32(0.0)).astype(jnp.bfloat16)
    lat_width = latent.shape[1]
    latent_out = (
        latent.reshape(tok_rows, spread, lat_width)
        .transpose(1, 0, 2)
        .reshape(1, tok_rows * spread, lat_width)
    )
    every_layer = lax.all_gather(latent[None], "layer", axis=0, tiled=True)
    keep_mask = (lax.iota(jnp.int32, layers) <= layer_now).astype(jnp.bfloat16)
    stacked = every_layer * keep_mask[:, None, None]
    sources = [which for which in range(layers)]
    latent_cat = jnp.concatenate([stacked[which] for which in range(layers)], axis=1)
    weight_cat = jnp.concatenate(
        [choose_source(dec_weight[0], sources[which], layers) for which in range(layers)], axis=0
    )
    partial_value = jnp.dot(hidden, down_weight[0], preferred_element_type=jnp.float32)
    partial_value = partial_value - jnp.dot(
        latent_cat, weight_cat, preferred_element_type=jnp.float32
    )
    summed = lax.psum_scatter(
        partial_value.reshape(tok_rows, spread * width),
        ("dp", "mp"),
        scatter_dimension=1,
        tiled=True,
    )
    error_out = summed.astype(jnp.bfloat16).reshape(1, tok_rows, -1)
    return (error_out, latent_out)


def solution(mesh):
    return jax.shard_map(
        body,
        mesh=mesh,
        in_specs=(
            P("layer", "dp", "mp"),
            P("layer", None, ("dp", "mp")),
            P("layer", None, ("dp", "mp")),
            P("layer", ("dp", "mp"), None),
            P("layer", None, ("dp", "mp")),
            P("layer", ("dp", "mp")),
            P("layer", None, ("dp", "mp"), None),
        ),
        out_specs=(P("layer", "dp", "mp"), P("layer", None, ("dp", "mp"))),
        check_vma=False,
    )
```

profile of v0, /device:TPU:1, one launch (start us, length us, event | category | flops | bytes accessed | tf_op | source)
XLA Modules:
  0.0 725.2 jit_solution(13167802963294468820)
XLA Ops:
  7.2 0.0 copy-start
  7.2 0.0 copy-start.3
  7.2 0.0 reduce-scatter.4.cloned.1.call-start
  7.3 0.8 copy.15
  8.1 75.4 %all_gather.9 = bf16[1,32,2048]{1,0,2:T(2,128)(2,1)S(1)} all-gather(bf16[1,32,64]{1,0,2:T(2,128)(2,1)S(1)} %copy.15), channel_id=1, replica_groups=mesh['layer'=4,'dp'=4,'mp'=32] {'mp'}, dimensions={2}, use_global_device_ids=true | all-gather | bytes 135168 | tf_op jit(solution)/shard_map/all_gather | solution.py:14
  83.5 0.5 copy.16
  84.0 0.0 copy-start.1
  84.0 0.0 copy-start.2
  84.1 20.7 %all-gather = bf16[1,32,8192]{2,1,0:T(8,128)(2,1)S(1)} all-gather(bf16[1,32,2048]{2,1,0:T(8,128)(2,1)S(1)} %copy.16), channel_id=2, replica_groups=mesh['layer'=4,'dp'=4,'mp'=32] {'dp'}, dimensions={2}, use_global_device_ids=true | all-gather | bytes 655360 | tf_op jit(solution)/shard_map/all_gather | solution.py:17
  104.7 0.4 reshape.36
  105.1 1.2 fusion.15
  106.4 0.0 copy-done
  106.4 0.0 copy-done.3
  106.4 0.3 fusion.8
  106.7 10.0 %all-gather.1 = bf16[512,128]{1,0:T(8,128)(2,1)S(1)} all-gather(bf16[128,128]{1,0:T(8,128)(2,1)S(1)} %fusion.8), channel_id=3, replica_groups=mesh['layer'=4,'dp'=4,'mp'=32] {'layer'}, dimensions={0}, use_global_device_ids=true | all-gather | bytes 163840 | tf_op jit(solution)/shard_map/all_gather | solution.py:33
  116.7 0.1 broadcast_multiply_fusion
  116.8 2.7 slice_bitcast_fusion.3
  119.6 0.0 copy-done.1
  119.6 0.0 copy-done.2
  119.6 0.8 fusion.10
  120.4 1.8 convolution_subtract_fusion
  122.2 0.5 reshape.37
  122.7 2.6 copy.18
  125.4 0.0 reduce-scatter.4.cloned.1.call-update
  125.4 0.6 copy.17
  126.0 590.9 %reduce-scatter.4.cloned.1.call-done = f32[64,32]{1,0:T(8,128)} async-done(((f32[8192,32]{1,0:T(8,128)}), f32[64,32]{1,0:T(8,128)}) %reduce-scatter.4.cloned.1.call-update) | async-done | bytes 8208
  716.9 1.4 copy.19
  (2 shorter events, 0.0 us)
Async XLA Ops:
  7.2 99.2 %copy-start = (bf16[1,2048,128]{2,1,0:T(8,128)(2,1)S(1)}, bf16[1,2048,128]{2,1,0:T(8,128)(2,1)}, u32[]{:S(2)}) copy-start(bf16[1,2048,128]{2,1,0:T(8,128)(2,1)} %param.11) | copy-start | bytes 1572868
  7.2 99.2 %copy-start.3 = (f32[1,128]{1,0:T(1,128)S(1)}, f32[1,128]{1,0:T(1,128)}, u32[]{:S(2)}) copy-start(f32[1,128]{1,0:T(1,128)} %param.12) | copy-start | bytes 1540
  7.2 709.7 %reduce-scatter.4.cloned.1.call-start = ((), (), s32[]{:S(2)}) async-start(), calls=%async_computation.1 | async-start | bytes 4227072
  84.0 35.5 %copy-start.1 = (bf16[1,64,2048]{2,1,0:T(8,128)(2,1)S(1)}, bf16[1,64,2048]{2,1,0:T(8,128)(2,1)}, u32[]{:S(2)}) copy-start(bf16[1,64,2048]{2,1,0:T(8,128)(2,1)} %param.10) | copy-start | bytes 786436
  84.0 35.5 %copy-start.2 = (bf16[1,2048,64]{1,2,0:T(8,128)(2,1)S(1)}, bf16[1,2048,64]{1,2,0:T(8,128)(2,1)}, u32[]{:S(2)}) copy-start(bf16[1,2048,64]{1,2,0:T(8,128)(2,1)} %param.9) | copy-start | bytes 786436
Sparse Core Ops, SparseCore 0:
  125.5 591.3 reduce-scatter.3
where the time goes:
time: 725 us
  waiting for transfers between devices  591 us (82%)
  blocking collectives  106 us (15%)
  between operations  14.1 us (2%)
  local copies, waits for them, and re-layouts  9.71 us (1%)
    unnamed x2, waiting for transfers between devices  591 us
    all_gather x1, blocking collectives, body(): features_full = lax.all_gather(mlp_in, 'mp', axis=2, tiled=True)  75.4 us
    all_gather x1, blocking collectives, body(): lax.all_gather(features_full.reshape(tok_rows, 1, width), 'dp', axis=1, t...  20.7 us
  transfers between devices with their start and end apart: 1, of which 1 were waited for; matrix products, arithmetic and copies ran while one was open for 0% of the time, Pallas kernels for 0%

commit v1 on v0

--- a/solution.py
+++ b/solution.py
@@ -11,7 +11,9 @@
 def body(mlp_in, gate_weight, up_weight, down_weight, enc_weight, enc_bias, dec_weight):
     layer_now = lax.axis_index("layer")
     layers = lax.axis_size("layer")
-    features_full = lax.all_gather(mlp_in, "mp", axis=2, tiled=True)
+    features_full = jnp.concatenate(
+        lax.all_to_all(jnp.stack([mlp_in] * lax.axis_size("mp")), "mp", 0, 0), axis=2
+    )
     tok_rows = features_full.shape[1]
     width = features_full.shape[2]
     gathered = lax.all_gather(features_full.reshape(tok_rows, 1, width), "dp", axis=1, tiled=True)

time: 725 us -> 665 us (0.917)
  blocking collectives: 106 us -> 20.1 us
  starting transfers between devices: 0.04 us -> 18.5 us
    all_gather x1 -> x0, blocking collectives: 75.4 us -> none  [body(): features_full = lax.all_gather(mlp_in, 'mp', axis=2, tiled=True)]
    all_to_all x0 -> x1, starting transfers between devices: none -> 18.5 us  [body(): lax.all_to_all(jnp.stack([mlp_in] * lax.axis_size('mp')), 'mp', 0, 0)]
    all_to_all x0 -> x1, waiting for transfers between devices: none -> 11.9 us  [body(): lax.all_to_all(jnp.stack([mlp_in] * lax.axis_size('mp')), 'mp', 0, 0)]
    all_gather x1, blocking collectives: 20.7 us -> 10.1 us  [body(): lax.all_gather(features_full.reshape(tok_rows, 1, width), 'dp', axis=1, t...]
  transfers between devices with their start and end apart: 1 -> 2, of which waited for: 1 -> 2; matrix products, arithmetic and copies ran while one was open for 0% -> 1% of each run, Pallas kernels for 0% -> 0%
where the time goes in v1:
time: 665 us
  waiting for transfers between devices  598 us (90%)
  blocking collectives  20.1 us (3%)
  starting transfers between devices  18.5 us (3%)
  between operations  14.2 us (2%)
  local copies, waits for them, and re-layouts  10.7 us (2%)
    unnamed x2, waiting for transfers between devices  586 us
    all_to_all x1, starting transfers between devices, body(): lax.all_to_all(jnp.stack([mlp_in] * lax.axis_size('mp')), 'mp', 0, 0)  18.5 us
  transfers between devices with their start and end apart: 2, of which 2 were waited for; matrix products, arithmetic and copies ran while one was open for 1% of the time, Pallas kernels for 0%

profile of v1, /device:TPU:1, one launch (start us, length us, event | category | flops | bytes accessed | tf_op | source)
XLA Modules:
  0.0 665.0 jit_solution(835939855945891386)
XLA Ops:
  7.2 0.0 copy-start
  7.2 0.8 stack.2
  8.0 0.8 reshape.47
  8.8 18.5 %all-to-all-start = ((bf16[32,2,1024]{2,1,0:T(2,128)(2,1)}), bf16[32,2,1024]{2,1,0:T(2,128)(2,1)S(1)}, u32[]{:S(2)}, u32[]{:S(2)}) async-start(bf16[32,2,1024]{2,1,0:T(2,128)(2,1)} %reshape.47), calls=%async_computation | async-start | bytes 262144 | tf_op jit(solution)/shard_map/all_to_all | solution.py:15
  27.3 0.0 copy-start.1
  27.3 0.0 reduce-scatter.4.cloned.1.call-start
  27.4 0.0 copy-start.4
  27.4 2.7 slice_bitcast_fusion.3
  30.1 0.0 copy-start.2
  30.1 0.0 copy-start.3
  30.1 11.9 %all-to-all-done = bf16[32,2,1024]{2,1,0:T(2,128)(2,1)S(1)} async-done(((bf16[32,2,1024]{2,1,0:T(2,128)(2,1)}), bf16[32,2,1024]{2,1,0:T(2,128)(2,1)S(1)}, u32[]{:S(2)}, u32[]{:S(2)}) %all-to-all-start) | async-done | bytes 131104 | tf_op jit(solution)/shard_map/all_to_all | solution.py:15
  42.1 0.2 reshape.48
  42.3 0.1 copy.13
  42.4 0.3 reshape_reshape.3
  42.7 10.1 %all_gather.6 = bf16[32,4,2048]{2,0,1:T(8,128)(2,1)S(1)} all-gather(bf16[32,1,2048]{2,0,1:T(8,128)(2,1)S(1)} %reshape_reshape.3), channel_id=1, replica_groups=mesh['layer'=4,'dp'=4,'mp'=32] {'dp'}, dimensions={1}, use_global_device_ids=true | all-gather | bytes 655360 | tf_op jit(solution)/shard_map/all_gather | solution.py:19
  52.7 0.4 copy.14
  53.2 0.1 reshape.39
  53.3 0.0 copy-done.1
  53.3 0.3 fusion.15
  53.6 0.0 copy-done
  53.6 0.0 copy-done.4
  53.6 0.3 fusion.8
  53.9 10.1 %all-gather = bf16[512,128]{1,0:T(8,128)(2,1)S(1)} all-gather(bf16[128,128]{1,0:T(8,128)(2,1)S(1)} %fusion.8), channel_id=2, replica_groups=mesh['layer'=4,'dp'=4,'mp'=32] {'layer'}, dimensions={0}, use_global_device_ids=true | all-gather | bytes 163840 | tf_op jit(solution)/shard_map/all_gather | solution.py:35
  64.0 0.1 broadcast_multiply_fusion
  64.1 0.0 copy-done.2
  64.1 0.0 copy-done.3
  64.1 0.8 fusion.10
  64.9 1.8 convolution_subtract_fusion
  66.7 0.5 reshape.40
  67.2 2.7 copy.16
  69.9 0.0 reduce-scatter.4.cloned.1.call-update
  69.9 0.6 copy.15
  70.5 586.2 %reduce-scatter.4.cloned.1.call-done = f32[64,32]{1,0:T(8,128)} async-done(((f32[8192,32]{1,0:T(8,128)}), f32[64,32]{1,0:T(8,128)}) %reduce-scatter.4.cloned.1.call-update) | async-done | bytes 8208
  656.7 1.4 copy.17
  (2 shorter events, 0.0 us)
Async XLA Ops:
  7.2 46.4 %copy-start = (bf16[1,2048,128]{2,1,0:T(8,128)(2,1)S(1)}, bf16[1,2048,128]{2,1,0:T(8,128)(2,1)}, u32[]{:S(2)}) copy-start(bf16[1,2048,128]{2,1,0:T(8,128)(2,1)} %param.11) | copy-start | bytes 1572868
  8.8 33.2 %all-to-all-start = ((bf16[32,2,1024]{2,1,0:T(2,128)(2,1)}), bf16[32,2,1024]{2,1,0:T(2,128)(2,1)S(1)}, u32[]{:S(2)}, u32[]{:S(2)}) async-start(bf16[32,2,1024]{2,1,0:T(2,128)(2,1)} %reshape.47), calls=%async_computation | async-start | bytes 262144 | tf_op jit(solution)/shard_map/all_to_all | solution.py:15
  27.3 26.0 %copy-start.1 = (bf16[1,2048,64]{1,2,0:T(8,128)(2,1)S(1)}, bf16[1,2048,64]{1,2,0:T(8,128)(2,1)}, u32[]{:S(2)}) copy-start(bf16[1,2048,64]{1,2,0:T(8,128)(2,1)} %param.8) | copy-start | bytes 786436
  27.3 629.4 %reduce-scatter.4.cloned.1.call-start = ((), (), s32[]{:S(2)}) async-start(), calls=%async_computation.2 | async-start | bytes 4227072
  27.4 26.2 %copy-start.4 = (f32[1,128]{1,0:T(1,128)S(1)}, f32[1,128]{1,0:T(1,128)}, u32[]{:S(2)}) copy-start(f32[1,128]{1,0:T(1,128)} %param.12) | copy-start | bytes 1540
  30.1 34.0 %copy-start.2 = (bf16[1,64,2048]{2,1,0:T(8,128)(2,1)S(1)}, bf16[1,64,2048]{2,1,0:T(8,128)(2,1)}, u32[]{:S(2)}) copy-start(bf16[1,64,2048]{2,1,0:T(8,128)(2,1)} %param.10) | copy-start | bytes 786436
  30.1 34.0 %copy-start.3 = (bf16[1,2048,64]{1,2,0:T(8,128)(2,1)S(1)}, bf16[1,2048,64]{1,2,0:T(8,128)(2,1)}, u32[]{:S(2)}) copy-start(bf16[1,2048,64]{1,2,0:T(8,128)(2,1)} %param.9) | copy-start | bytes 786436
Sparse Core Ops, SparseCore 0:
  70.0 586.6 reduce-scatter.3
